TPU v7x, 256 devices: a whole 4x4x8 slice. The times are simulated.
256 devices in a mesh: snap: 8 (over y, core), vtx: 32 (over z, x).
Axes of the slice: x: 4, y: 4, z: 8, core: 2. Of those that a mesh axis runs over, the one named last changes fastest.
Arguments:
- features: bfloat16 [16, 32768, 128], P('snap', 'vtx'), may hold values from -6 to 6
- tile_vals: bfloat16 [16, 256, 16, 128, 128], P('snap', 'vtx'), may hold values from -0.25 to 0.25
- tile_cols: int32 [16, 256, 16], P('snap', 'vtx'), may hold values from 0 to 255, as said below
- tile_count: int32 [16, 256], P('snap', 'vtx'), may hold values from 1 to 16
- gcn_weight: bfloat16 [128, 128], replicated, may hold values from -0.5 to 0.5
- gcn_bias: float32 [128], replicated, may hold values from -3 to 3
- input_weight: bfloat16 [128, 512], replicated, may hold values from -0.5 to 0.5
- recur_weight: bfloat16 [128, 512], replicated, may hold values from -0.5 to 0.5
- lstm_bias: float32 [512], replicated, may hold values from -4 to 4
- hidden_grad: bfloat16 [32, 1024, 16, 128], P('vtx', 'snap'), may hold values from -6 to 6
Outputs:
- hidden_states: bfloat16 [32, 1024, 16, 128], P('vtx', 'snap')
- grad_gcn_weight: float32 [128, 128], replicated
- grad_gcn_bias: float32 [128], replicated
- grad_input_weight: float32 [128, 512], replicated
- grad_recur_weight: float32 [128, 512], replicated
- grad_lstm_bias: float32 [512], replicated
Inputs may be any that keep to these rules, and one draw needn't show every extreme that they name: `tile_cols`: within one snapshot, the 16 slots of one row block name distinct column blocks, and all slots, live or not, of the row blocks j * 8 to (j + 1) * 8 - 1 together name at most one block of each group of 8 consecutive blocks.
All inputs are finite; a program needn't handle non-finite values.
Results may differ from a plain program's by a relative error of at most 0.0085.
Values may be sent and summed in bfloat16 or wider, within the bound.
No kernel may reach another device: no remote copies, remote signals or barrier semaphores. Data moves between devices by JAX's collectives and lax.ppermute only.
A program may use at most 128 MiB of HBM per device.

v0:
```python
import jax
import jax.numpy as jnp
from jax import lax
from jax.sharding import PartitionSpec as P


def silu_slope(grad_layer, pre_act):
    squeeze = jax.nn.sigmoid(pre_act)
    return (grad_layer.astype(jnp.float32) * squeeze * (1.0 + pre_act * (1.0 - squeeze))).astype(
        jnp.bfloat16
    )


def on_device(
    features,
    tile_vals,
    tile_cols,
    tile_count,
    gcn_weight,
    gcn_bias,
    input_weight,
    recur_weight,
    lstm_bias,
    hidden_grad,
):
    steps_dev, local_verts, feat_width = features.shape
    tile_size = tile_vals.shape[3]
    hidden_size = recur_weight.shape[0]
    live_mask = lax.broadcasted_iota(jnp.int32, tile_cols.shape, 2) < tile_count[:, :, None]
    snap_iota = lax.broadcasted_iota(jnp.int32, tile_cols.shape, 0)
    gathered = lax.all_gather(features, "vtx", axis=1, tiled=True)
    whole_blocks = gathered.reshape(steps_dev, -1, tile_size, feat_width)
    fetched_blocks = whole_blocks[snap_iota, tile_cols]
    blocks_used = jnp.where(
        live_mask[..., None, None], fetched_blocks, jnp.zeros_like(fetched_blocks)
    )
    summed = jnp.einsum(
        "svmij,svmjf->svif", tile_vals, blocks_used, preferred_element_type=jnp.float32
    )
    aggregated = summed.astype(jnp.bfloat16).reshape(steps_dev * local_verts, feat_width)
    pre_act = jnp.dot(aggregated, gcn_weight, preferred_element_type=jnp.float32) + gcn_bias
    layer_out = (
        jax.nn.silu(pre_act).astype(jnp.bfloat16).reshape(steps_dev, local_verts, feat_width)
    )
    vertex_inputs = lax.all_to_all(layer_out, "snap", split_axis=1, concat_axis=0, tiled=True)
    total_steps, vertex_rows, _ = vertex_inputs.shape
    flat_inputs = vertex_inputs.reshape(total_steps * vertex_rows, feat_width)
    input_gates = (
        jnp.dot(flat_inputs, input_weight, preferred_element_type=jnp.float32) + lstm_bias
    ).reshape(total_steps, vertex_rows, 4 * hidden_size)

    def advance(carried, gates_step):
        cell_state, last_out = carried
        pre_gates = gates_step + jnp.dot(last_out, recur_weight, preferred_element_type=jnp.float32)
        gate_in = jax.nn.sigmoid(pre_gates[:, :hidden_size])
        gate_keep = jax.nn.sigmoid(pre_gates[:, hidden_size : 2 * hidden_size])
        gate_new = jnp.tanh(pre_gates[:, 2 * hidden_size : 3 * hidden_size])
        gate_out = jax.nn.sigmoid(pre_gates[:, 3 * hidden_size :])
        cell_state = gate_keep * cell_state + gate_in * gate_new
        new_out = (gate_out * jnp.tanh(cell_state)).astype(jnp.bfloat16)
        return ((cell_state, new_out), (pre_gates, cell_state, new_out))

    zero_cell = jnp.zeros((vertex_rows, hidden_size), jnp.float32)
    start = (zero_cell, jnp.zeros((vertex_rows, hidden_size), jnp.bfloat16))
    _, (all_pre, all_cells, all_outs) = lax.scan(advance, start, input_gates)
    prev_cells = jnp.concatenate([zero_cell[None], all_cells[:-1]], axis=0)
    prev_outs = jnp.concatenate([start[1][None], all_outs[:-1]], axis=0)
    grad_outs = jnp.transpose(hidden_grad[0], (1, 0, 2)).astype(jnp.float32)

    def retreat(carried, step_items):
        grad_cell, grad_back = carried
        pre_gates, cell_state, prev_cell, grad_out = step_items
        gate_in = jax.nn.sigmoid(pre_gates[:, :hidden_size])
        gate_keep = jax.nn.sigmoid(pre_gates[:, hidden_size : 2 * hidden_size])
        gate_new = jnp.tanh(pre_gates[:, 2 * hidden_size : 3 * hidden_size])
        gate_out = jax.nn.sigmoid(pre_gates[:, 3 * hidden_size :])
        squash = jnp.tanh(cell_state)
        grad_total = grad_out + grad_back
        grad_cell = grad_cell + grad_total * gate_out * (1.0 - squash * squash)
        grad_gates = jnp.concatenate(
            [
                grad_cell * gate_new * gate_in * (1.0 - gate_in),
                grad_cell * prev_cell * gate_keep * (1.0 - gate_keep),
                grad_cell * gate_in * (1.0 - gate_new * gate_new),
                grad_total * squash * gate_out * (1.0 - gate_out),
            ],
            axis=1,
        ).astype(jnp.bfloat16)
        grad_back = jnp.einsum(
            "rg,hg->rh", grad_gates, recur_weight, preferred_element_type=jnp.float32
        )
        return ((grad_cell * gate_keep, grad_back), grad_gates)

    _, all_grad_gates = lax.scan(
        retreat, (zero_cell, zero_cell), (all_pre, all_cells, prev_cells, grad_outs), reverse=True
    )
    flat_gates = all_grad_gates.reshape(total_steps * vertex_rows, 4 * hidden_size)
    grad_input = jnp.einsum(
        "rf,rg->fg", flat_inputs, flat_gates, preferred_element_type=jnp.float32
    )
    grad_recur = jnp.einsum(
        "rh,rg->hg",
        prev_outs.reshape(total_steps * vertex_rows, hidden_size),
        flat_gates,
        preferred_element_type=jnp.float32,
    )
    grad_bias = jnp.sum(flat_gates.astype(jnp.float32), axis=0)
    grad_layer = jnp.einsum(
        "rg,fg->rf", flat_gates, input_weight, preferred_element_type=jnp.float32
    ).astype(jnp.bfloat16)
    grad_snap = lax.all_to_all(
        grad_layer.reshape(total_steps, vertex_rows, feat_width),
        "snap",
        split_axis=0,
        concat_axis=1,
        tiled=True,
    )
    grad_snap = grad_snap.reshape(steps_dev * local_verts, feat_width)
    grad_pre = silu_slope(grad_snap, pre_act)
    grad_gcn = jnp.einsum("rf,rg->fg", aggregated, grad_pre, preferred_element_type=jnp.float32)
    grad_gbias = jnp.sum(grad_pre.astype(jnp.float32), axis=0)
    grad_gcn, grad_gbias, grad_input, grad_recur, grad_bias = lax.psum(
        (grad_gcn, grad_gbias, grad_input, grad_recur, grad_bias), ("snap", "vtx")
    )
    hidden_states = jnp.transpose(all_outs, (1, 0, 2))[None]
    return (hidden_states, grad_gcn, grad_gbias, grad_input, grad_recur, grad_bias)


def solution(mesh):
    return jax.shard_map(
        on_device,
        mesh=mesh,
        in_specs=(
            P("snap", "vtx", None),
            P("snap", "vtx", None, None, None),
            P("snap", "vtx", None),
            P("snap", "vtx"),
            P(),
            P(),
            P(),
            P(),
            P(),
            P("vtx", "snap", None, None),
        ),
        out_specs=(P("vtx", "snap", None, None), P(), P(), P(), P(), P()),
        check_vma=False,
    )
```

profile of v0, /device:TPU:1, one launch (start us, length us, event | category | flops | bytes accessed | tf_op | source)
XLA Modules:
  0.0 570.2 jit_solution(6579747021246747212)
XLA Ops:
  9.5 145.1 %all-gather.2.cloned.1.call-done = bf16[2,32768,128]{2,1,0:T(8,128)(2,1)} async-done(((bf16[2,1024,128]{2,1,0:T(8,128)(2,1)}), bf16[2,32768,128]{2,1,0:T(8,128)(2,1)}) %all-gather.2.cloned.1.call-update) | async-done | bytes 16777232 | tf_op jit(solution)/shard_map/all_gather | solution.py:31
  154.6 15.9 %gather_fusion = bf16[256,128,128]{2,1,0:T(8,128)(2,1)} fusion(bf16[2,256,128,128]{3,2,1,0:T(8,128)(2,1)} %bitcast.136, s32[256]{0:T(256)S(1)} %reshape.144), kind=kCustom, calls=%fused_computation | custom fusion | bytes 16779264 | tf_op jit(solution)/shard_map/gather | solution.py:33
  170.4 8.2 %fusion.53 = bf16[2,8,128,128]{2,3,1,0:T(8,128)(2,1)S(1)} fusion(bf16[2,8,16,128,128]{4,3,2,1,0:T(8,128)(2,1)} %param.15, bf16[2,8,16,128,128]{4,3,2,1,0:T(8,128)(2,1)} %bitcast.132, pred[2,8,16]{2,1,0:T(8,128)(4,1)S(1)} %iota_compare_fusion), kind=kOutput, calls=%fused_computation.77 | convolution fusion | flops 1078198272 | bytes 17301760 | tf_op jit(solution)/shard_map/svmij,svmjf->svif/dot_general | solution.py:37
  182.2 5.3 all-to-all-start
  188.6 8.3 %all-to-all-done = bf16[2,1024,128]{2,0,1:T(2,128)(2,1)S(1)} async-done(((bf16[2,1024,128]{2,0,1:T(2,128)(2,1)}), bf16[2,1024,128]{2,0,1:T(2,128)(2,1)S(1)}, u32[]{:S(2)}, u32[]{:S(2)}) %all-to-all-start) | async-done | bytes 524320 | tf_op jit(solution)/shard_map/all_to_all | solution.py:45
  197.1 2.6 convolution_add_fusion.1
  199.7 41.2 %while.38 = (s32[]{:T(128)}, f32[128,128]{1,0:T(8,128)S(1)}, bf16[128,128]{1,0:T(8,128)(2,1)S(1)}, f32[16,128,512]{2,1,0:T(8,128)}, f32[16,128,128]{2,1,0:T(8,12...) while((s32[]{:T(128)}, f32[128,128]{1,0:T(8,128)S(1)}, ...), condition=%wide.region_1.2_spmd.clone, body=%wide.region_0.1_spmd.clone.sunk | while | flops 17104900 | bytes 1541236 | solution.py:65
  199.7 1.9 bitcast_dynamic-update-slice_fusion.6
  202.3 1.8 bitcast_dynamic-update-slice_fusion.6
  204.9 1.9 bitcast_dynamic-update-slice_fusion.6
  207.5 1.8 bitcast_dynamic-update-slice_fusion.6
  210.0 1.8 bitcast_dynamic-update-slice_fusion.6
  212.6 1.8 bitcast_dynamic-update-slice_fusion.6
  215.2 1.8 bitcast_dynamic-update-slice_fusion.6
  217.7 1.8 bitcast_dynamic-update-slice_fusion.6
  220.3 1.9 bitcast_dynamic-update-slice_fusion.6
  222.9 1.8 bitcast_dynamic-update-slice_fusion.6
  225.5 1.8 bitcast_dynamic-update-slice_fusion.6
  228.0 1.8 bitcast_dynamic-update-slice_fusion.6
  230.6 1.8 bitcast_dynamic-update-slice_fusion.6
  233.2 1.8 bitcast_dynamic-update-slice_fusion.6
  235.7 1.9 bitcast_dynamic-update-slice_fusion.6
  238.3 1.9 bitcast_dynamic-update-slice_fusion.6
  242.5 49.4 %while.39 = (s32[]{:T(128)}, f32[128,128]{1,0:T(8,128)S(1)}, f32[128,128]{1,0:T(8,128)S(1)}, bf16[16,128,512]{2,1,0:T(8,128)(2,1)S(1)}, f32[16,128,128]{2,1,0:T(...) while((s32[]{:T(128)}, f32[128,128]{1,0:T(8,128)S(1)}, ...), condition=%wide.region_3.4_spmd.clone, body=%wide.region_2.3_spmd.clone.sunk | while | flops 18481156 | bytes 2162843 | solution.py:94
  291.9 2.1 copy.34
  295.5 4.3 all-to-all-start.1
  299.8 2.2 convolution_bitcast_fusion
  303.1 6.1 %all-to-all-done.1 = bf16[16,128,128]{2,1,0:T(8,128)(2,1)S(1)} async-done(((bf16[16,128,128]{2,1,0:T(8,128)(2,1)}), bf16[16,128,128]{2,1,0:T(8,128)(2,1)S(1)}, u32[]{:S(2)}, u32[]{:S(2)}) %all-to-all-start.1) | async-done | bytes 524320 | tf_op jit(solution)/shard_map/all_to_all | solution.py:111
  313.4 73.9 %all-reduce.2 = (f32[128]{0:T(128)}, f32[512]{0:T(512)}) all-reduce(f32[128]{0:T(128)S(1)} %get-tuple-element.334, f32[512]{0:T(512)S(1)} %convert_reduce_fusion), channel_id=1, replica_groups=mesh['snap'=8,'vtx'=32] {'snap','vtx'}, use_global_device_ids=true, to_apply=%region_6.7 | all-reduce | flops 640 | bytes 5120 | tf_op jit(solution)/shard_map/psum | solution.py:122
  387.4 171.2 %all-reduce.6.cloned.1.call-done = (f32[128,128]{1,0:T(8,128)}, f32[128,512]{1,0:T(8,128)}, f32[128,512]{1,0:T(8,128)}) async-done(((f32[128,128]{1,0:T(8,128)}, f32[128,512]{1,0:T(8,128)}, f32[128,512]{1,0:T(8,128)}), (f32[128,128]{1,0:T(8,128)}, f32[128,512]{1,0:T(8,128)}, f32[128,512]{1,0:T(8,128)})) %all-reduce.6.cloned.1.call-update) | async-done | bytes 589840 | tf_op jit(solution)/shard_map/psum | solution.py:122
  560.0 1.7 copy.77
  561.7 1.7 copy.78
  (165 shorter events, 77.0 us)
Async XLA Ops:
  7.2 189.9 %copy-start = (bf16[128,512]{1,0:T(8,128)(2,1)S(1)}, bf16[128,512]{1,0:T(8,128)(2,1)}, u32[]{:S(2)}) copy-start(bf16[128,512]{1,0:T(8,128)(2,1)} %param.20) | copy-start | bytes 393220
  7.2 147.4 %all-gather.2.cloned.1.call-start = ((), (), s32[]{:S(2)}) async-start(), calls=%async_computation.2 | async-start | bytes 17301504 | tf_op jit(solution)/shard_map/all_gather | solution.py:31
  170.4 9.0 %copy-start.9 = (bf16[128,128]{1,0:T(8,128)(2,1)S(1)}, bf16[128,128]{1,0:T(8,128)(2,1)}, u32[]{:S(2)}) copy-start(bf16[128,128]{1,0:T(8,128)(2,1)} %param.18) | copy-start | bytes 98308
  170.4 9.0 %copy-start.10 = (f32[128]{0:T(128)S(1)}, f32[128]{0:T(128)}, u32[]{:S(2)}) copy-start(f32[128]{0:T(128)} %param.19) | copy-start | bytes 1540
  178.6 0.8 copy-start.6
  178.6 8.9 %copy-start.5 = (bf16[1,128,16,128]{3,2,1,0:T(8,128)(2,1)S(1)}, bf16[1,128,16,128]{3,2,1,0:T(8,128)(2,1)}, u32[]{:S(2)}) copy-start(bf16[1,128,16,128]{3,2,1,0:T(8,128)(2,1)} %param.23) | copy-start | bytes 1572868
  180.8 16.3 %copy-start.8 = (f32[512]{0:T(512)S(1)}, f32[512]{0:T(512)}, u32[]{:S(2)}) copy-start(f32[512]{0:T(512)} %param.22) | copy-start | bytes 6148
  182.2 14.8 %all-to-all-start = ((bf16[2,1024,128]{2,0,1:T(2,128)(2,1)}), bf16[2,1024,128]{2,0,1:T(2,128)(2,1)S(1)}, u32[]{:S(2)}, u32[]{:S(2)}) async-start(bf16[2,1024,128]{2,0,1:T(2,128)(2,1)} %copy.28), calls=%async_computation | async-start | bytes 1048576 | tf_op jit(solution)/shard_map/all_to_all | solution.py:45
  187.5 12.2 %copy-start.1 = (bf16[128,512]{1,0:T(8,128)(2,1)S(1)}, bf16[128,512]{1,0:T(8,128)(2,1)}, u32[]{:S(2)}) copy-start(bf16[128,512]{1,0:T(8,128)(2,1)} %param.21) | copy-start | bytes 393220
  240.9 1.3 copy-start.3
  295.5 13.8 %all-to-all-start.1 = ((bf16[16,128,128]{2,1,0:T(8,128)(2,1)}), bf16[16,128,128]{2,1,0:T(8,128)(2,1)S(1)}, u32[]{:S(2)}, u32[]{:S(2)}) async-start(bf16[16,128,128]{2,1,0:T(8,128)(2,1)} %bitcast.143), calls=%async_computation.1 | async-start | bytes 1048576 | tf_op jit(solution)/shard_map/all_to_all | solution.py:111
  299.8 258.8 %all-reduce.6.cloned.1.call-start = ((), (), s32[]{:S(2)}) async-start(), calls=%async_computation.3 | async-start | bytes 1179648 | tf_op jit(solution)/shard_map/psum | solution.py:122
  303.1 8.8 %copy-start.2 = (bf16[16,128,128]{2,1,0:T(8,128)(2,1)S(1)}, bf16[16,128,128]{2,1,0:T(8,128)(2,1)}, u32[]{:S(2)}) copy-start(bf16[16,128,128]{2,1,0:T(8,128)(2,1)} %get-tuple-element.229) | copy-start | bytes 1572868
  309.3 1.2 copy-start.4
  309.3 1.7 copy-start.7
Sparse Core Ops, SparseCore 0:
  10.6 143.9 all-gather.1
  312.1 246.4 all-reduce.5
where the time goes:
time: 573 us; the launch traced here: 570 us
  waiting for transfers between devices  331 us (58%)
  blocking collectives  73.9 us (13%)
  matrix products  50.5 us (9%)
  other arithmetic  44.9 us (8%)
  local copies, waits for them, and re-layouts  44.5 us (8%)
  between operations  14.2 us (2%)
  starting transfers between devices  9.64 us (2%)
    psum x1, waiting for transfers between devices, on_device(): lax.psum((grad_gcn, grad_gbias, grad_input, grad_recur, grad_bias), ('sna...  171 us
    all_gather x1, waiting for transfers between devices, on_device(): gathered = lax.all_gather(features, 'vtx', axis=1, tiled=True)  145 us
    psum x1, blocking collectives, on_device(): lax.psum((grad_gcn, grad_gbias, grad_input, grad_recur, grad_bias), ('sna...  73.9 us
    another operation x32, other arithmetic  29.8 us
    dot_general x16, matrix products, advance(): jnp.dot(last_out, recur_weight, preferred_element_type=jnp.float32)  29.5 us
    gather x1, local copies, waits for them, and re-layouts, on_device(): fetched_blocks = whole_blocks[snap_iota, tile_cols]  15.9 us
    squeeze x16, local copies, waits for them, and re-layouts, on_device(): _, (all_pre, all_cells, all_outs) = lax.scan(advance, start, input_gates)  15.6 us
  transfers between devices with their start and end apart: 4, of which 4 were waited for; matrix products, arithmetic and copies ran while one was open for 1% of the time, Pallas kernels for 0%

commit v1 on v0

--- a/solution.py
+++ b/solution.py
@@ -120,7 +120,7 @@
     grad_gcn = jnp.einsum("rf,rg->fg", aggregated, grad_pre, preferred_element_type=jnp.float32)
     grad_gbias = jnp.sum(grad_pre.astype(jnp.float32), axis=0)
     grad_gcn, grad_gbias, grad_input, grad_recur, grad_bias = lax.psum(
-        (grad_gcn, grad_gbias, grad_input, grad_recur, grad_bias), ("snap", "vtx")
+        lax.psum((grad_gcn, grad_gbias, grad_input, grad_recur, grad_bias), "snap"), "vtx"
     )
     hidden_states = jnp.transpose(all_outs, (1, 0, 2))[None]
     return (hidden_states, grad_gcn, grad_gbias, grad_input, grad_recur, grad_bias)

time: 573 us -> 550 us (0.960)
  waiting for transfers between devices: 331 us -> 291 us
  local copies, waits for them, and re-layouts: 44.5 us -> 55.5 us
    psum x1 -> x2, waiting for transfers between devices: 171 us -> 131 us  [the longest x1 70.7 us: on_device(): lax.psum(lax.psum((grad_gcn, grad_gbias, grad_input, grad_recur, grad_bia...]
    dynamic_update_slice x16, local copies, waits for them, and re-layouts: 0.13 us -> 10 us  [on_device(): _, (all_pre, all_cells, all_outs) = lax.scan(advance, start, input_gates)]
    psum x1 -> x2, blocking collectives: 73.9 us -> 75.9 us  [the longest x1 61.5 us: on_device(): lax.psum(lax.psum((grad_gcn, grad_gbias, grad_input, grad_recur, grad_bia...]
  transfers between devices with their start and end apart: 4 -> 5, of which waited for: 4 -> 5; matrix products, arithmetic and copies ran while one was open for 1% -> 1% of each run, Pallas kernels for 0% -> 0%
where the time goes in v1:
time: 550 us; the launch traced here: 543 us
  waiting for transfers between devices  291 us (53%)
  blocking collectives  75.9 us (14%)
  local copies, waits for them, and re-layouts  55.5 us (10%)
  matrix products  51.4 us (9%)
  other arithmetic  44.9 us (8%)
  between operations  13.9 us (3%)
  starting transfers between devices  9.66 us (2%)
    all_gather x1, waiting for transfers between devices, on_device(): gathered = lax.all_gather(features, 'vtx', axis=1, tiled=True)  145 us
    psum x1, waiting for transfers between devices, on_device(): lax.psum(lax.psum((grad_gcn, grad_gbias, grad_input, grad_recur, grad_bia...  70.7 us
    psum x1, blocking collectives, on_device(): lax.psum(lax.psum((grad_gcn, grad_gbias, grad_input, grad_recur, grad_bia...  61.5 us
    psum x1, waiting for transfers between devices, on_device(): lax.psum((grad_gcn, grad_gbias, grad_input, grad_recur, grad_bias), 'snap')  59.9 us
    another operation x32, other arithmetic  29.8 us
    dot_general x16, matrix products, advance(): jnp.dot(last_out, recur_weight, preferred_element_type=jnp.float32)  29.4 us
    gather x1, local copies, waits for them, and re-layouts, on_device(): fetched_blocks = whole_blocks[snap_iota, tile_cols]  15.9 us
    squeeze x16, local copies, waits for them, and re-layouts, on_device(): _, (all_pre, all_cells, all_outs) = lax.scan(advance, start, input_gates)  15.6 us
  transfers between devices with their start and end apart: 5, of which 5 were waited for; matrix products, arithmetic and copies ran while one was open for 1% of the time, Pallas kernels for 0%

profile of v1, /device:TPU:1, one launch (start us, length us, event | category | flops | bytes accessed | tf_op | source)
XLA Modules:
  0.0 543.0 jit_solution(6394655240976964662)
XLA Ops:
  9.5 145.1 %all-gather.2.cloned.1.call-done = bf16[2,32768,128]{2,1,0:T(8,128)(2,1)} async-done(((bf16[2,1024,128]{2,1,0:T(8,128)(2,1)}), bf16[2,32768,128]{2,1,0:T(8,128)(2,1)}) %all-gather.2.cloned.1.call-update) | async-done | bytes 16777232 | tf_op jit(solution)/shard_map/all_gather | solution.py:31
  154.6 15.9 %gather_fusion = bf16[256,128,128]{2,1,0:T(8,128)(2,1)} fusion(bf16[2,256,128,128]{3,2,1,0:T(8,128)(2,1)} %bitcast.136, s32[256]{0:T(256)S(1)} %reshape.144), kind=kCustom, calls=%fused_computation | custom fusion | bytes 16779264 | tf_op jit(solution)/shard_map/gather | solution.py:33
  170.4 8.2 %fusion.53 = bf16[2,8,128,128]{2,3,1,0:T(8,128)(2,1)S(1)} fusion(bf16[2,8,16,128,128]{4,3,2,1,0:T(8,128)(2,1)} %param.15, bf16[2,8,16,128,128]{4,3,2,1,0:T(8,128)(2,1)} %bitcast.132, pred[2,8,16]{2,1,0:T(8,128)(4,1)S(1)} %iota_compare_fusion), kind=kOutput, calls=%fused_computation.77 | convolution fusion | flops 1078198272 | bytes 17301760 | tf_op jit(solution)/shard_map/svmij,svmjf->svif/dot_general | solution.py:37
  182.2 5.3 all-to-all-start
  188.6 8.3 %all-to-all-done = bf16[2,1024,128]{2,0,1:T(2,128)(2,1)S(1)} async-done(((bf16[2,1024,128]{2,0,1:T(2,128)(2,1)}), bf16[2,1024,128]{2,0,1:T(2,128)(2,1)S(1)}, u32[]{:S(2)}, u32[]{:S(2)}) %all-to-all-start) | async-done | bytes 524320 | tf_op jit(solution)/shard_map/all_to_all | solution.py:45
  197.1 2.7 convolution_add_fusion.1
  199.8 50.6 %while.38 = (s32[]{:T(128)}, f32[128,128]{1,0:T(8,128)S(1)}, bf16[128,128]{1,0:T(8,128)(2,1)S(1)}, f32[16,128,512]{2,1,0:T(8,128)}, f32[16,128,128]{2,1,0:T(8,12...) while((s32[]{:T(128)}, f32[128,128]{1,0:T(8,128)S(1)}, ...), condition=%wide.region_1.2_spmd.clone, body=%wide.region_0.1_spmd.clone.sunk | while | flops 17104900 | bytes 1541744 | solution.py:65
  199.8 1.8 bitcast_dynamic-update-slice_fusion.6
  206.1 1.8 bitcast_dynamic-update-slice_fusion.6
  209.2 1.8 bitcast_dynamic-update-slice_fusion.6
  212.4 1.9 bitcast_dynamic-update-slice_fusion.6
  215.6 1.8 bitcast_dynamic-update-slice_fusion.6
  218.8 1.8 bitcast_dynamic-update-slice_fusion.6
  221.9 1.8 bitcast_dynamic-update-slice_fusion.6
  225.1 1.8 bitcast_dynamic-update-slice_fusion.6
  228.3 1.8 bitcast_dynamic-update-slice_fusion.6
  231.4 1.8 bitcast_dynamic-update-slice_fusion.6
  234.6 1.8 bitcast_dynamic-update-slice_fusion.6
  237.8 1.8 bitcast_dynamic-update-slice_fusion.6
  240.9 1.8 bitcast_dynamic-update-slice_fusion.6
  244.1 1.9 bitcast_dynamic-update-slice_fusion.6
  247.2 1.8 bitcast_dynamic-update-slice_fusion.6
  253.0 49.4 %while.39 = (s32[]{:T(128)}, f32[128,128]{1,0:T(8,128)S(1)}, f32[128,128]{1,0:T(8,128)S(1)}, bf16[16,128,512]{2,1,0:T(8,128)(2,1)S(1)}, f32[16,128,128]{2,1,0:T(...) while((s32[]{:T(128)}, f32[128,128]{1,0:T(8,128)S(1)}, ...), condition=%wide.region_3.4_spmd.clone, body=%wide.region_2.3_spmd.clone.sunk | while | flops 18481156 | bytes 2162843 | solution.py:94
  302.5 2.1 copy.34
  306.0 4.3 all-to-all-start.1
  310.3 2.2 convolution_bitcast_fusion
  313.6 6.1 %all-to-all-done.1 = bf16[16,128,128]{2,1,0:T(8,128)(2,1)S(1)} async-done(((bf16[16,128,128]{2,1,0:T(8,128)(2,1)}), bf16[16,128,128]{2,1,0:T(8,128)(2,1)S(1)}, u32[]{:S(2)}, u32[]{:S(2)}) %all-to-all-start.1) | async-done | bytes 524320 | tf_op jit(solution)/shard_map/all_to_all | solution.py:111
  321.5 2.0 fusion.68
  323.6 59.9 %all-reduce.11.cloned.1.call-done = (f32[128,128]{1,0:T(8,128)}, f32[128,512]{1,0:T(8,128)}, f32[128,512]{1,0:T(8,128)}) async-done(((f32[128,128]{1,0:T(8,128)}, f32[128,512]{1,0:T(8,128)}, f32[128,512]{1,0:T(8,128)}), (f32[128,128]{1,0:T(8,128)}, f32[128,512]{1,0:T(8,128)}, f32[128,512]{1,0:T(8,128)})) %all-reduce.11.cloned.1.call-update) | async-done | bytes 589840 | tf_op jit(solution)/shard_map/psum | solution.py:123
  385.0 14.4 %all-reduce.4 = (f32[128]{0:T(128)S(1)}, f32[512]{0:T(512)S(1)}) all-reduce(f32[128]{0:T(128)S(1)} %get-tuple-element.339, f32[512]{0:T(512)S(1)} %convert_reduce_fusion), channel_id=1, replica_groups=mesh['snap'=8,'vtx'=32] {'snap'}, use_global_device_ids=true, to_apply=%region_7.8 | all-reduce | flops 640 | bytes 5120 | tf_op jit(solution)/shard_map/psum | solution.py:123
  399.3 61.5 %all-reduce.2 = (f32[128]{0:T(128)}, f32[512]{0:T(512)}) all-reduce(f32[128]{0:T(128)S(1)} %get-tuple-element.329, f32[512]{0:T(512)S(1)} %get-tuple-element.330), channel_id=1, replica_groups=mesh['snap'=8,'vtx'=32] {'vtx'}, use_global_device_ids=true, to_apply=%region_8.9 | all-reduce | flops 640 | bytes 5120 | tf_op jit(solution)/shard_map/psum | solution.py:122
  460.9 70.7 %all-reduce.9.cloned.1.call-done = (f32[128,128]{1,0:T(8,128)}, f32[128,512]{1,0:T(8,128)}, f32[128,512]{1,0:T(8,128)}) async-done(((f32[128,128]{1,0:T(8,128)}, f32[128,512]{1,0:T(8,128)}, f32[128,512]{1,0:T(8,128)}), (f32[128,128]{1,0:T(8,128)}, f32[128,512]{1,0:T(8,128)}, f32[128,512]{1,0:T(8,128)})) %all-reduce.9.cloned.1.call-update) | async-done | bytes 589840 | tf_op jit(solution)/shard_map/psum | solution.py:122
  (165 shorter events, 92.1 us)
Async XLA Ops:
  7.2 189.9 %copy-start = (bf16[128,512]{1,0:T(8,128)(2,1)S(1)}, bf16[128,512]{1,0:T(8,128)(2,1)}, u32[]{:S(2)}) copy-start(bf16[128,512]{1,0:T(8,128)(2,1)} %param.20) | copy-start | bytes 393220
  7.2 147.4 %all-gather.2.cloned.1.call-start = ((), (), s32[]{:S(2)}) async-start(), calls=%async_computation.2 | async-start | bytes 17301504 | tf_op jit(solution)/shard_map/all_gather | solution.py:31
  170.4 9.0 %copy-start.7 = (bf16[128,128]{1,0:T(8,128)(2,1)S(1)}, bf16[128,128]{1,0:T(8,128)(2,1)}, u32[]{:S(2)}) copy-start(bf16[128,128]{1,0:T(8,128)(2,1)} %param.18) | copy-start | bytes 98308
  170.4 9.0 %copy-start.8 = (f32[128]{0:T(128)S(1)}, f32[128]{0:T(128)}, u32[]{:S(2)}) copy-start(f32[128]{0:T(128)} %param.19) | copy-start | bytes 1540
  178.6 0.8 copy-start.5
  178.6 8.9 %copy-start.4 = (bf16[1,128,16,128]{3,2,1,0:T(8,128)(2,1)S(1)}, bf16[1,128,16,128]{3,2,1,0:T(8,128)(2,1)}, u32[]{:S(2)}) copy-start(bf16[1,128,16,128]{3,2,1,0:T(8,128)(2,1)} %param.23) | copy-start | bytes 1572868
  180.8 16.3 %copy-start.6 = (f32[512]{0:T(512)S(1)}, f32[512]{0:T(512)}, u32[]{:S(2)}) copy-start(f32[512]{0:T(512)} %param.22) | copy-start | bytes 6148
  182.2 14.8 %all-to-all-start = ((bf16[2,1024,128]{2,0,1:T(2,128)(2,1)}), bf16[2,1024,128]{2,0,1:T(2,128)(2,1)S(1)}, u32[]{:S(2)}, u32[]{:S(2)}) async-start(bf16[2,1024,128]{2,0,1:T(2,128)(2,1)} %copy.28), calls=%async_computation | async-start | bytes 1048576 | tf_op jit(solution)/shard_map/all_to_all | solution.py:45
  187.5 12.3 %copy-start.1 = (bf16[128,512]{1,0:T(8,128)(2,1)S(1)}, bf16[128,512]{1,0:T(8,128)(2,1)}, u32[]{:S(2)}) copy-start(bf16[128,512]{1,0:T(8,128)(2,1)} %param.21) | copy-start | bytes 393220
  306.0 13.8 %all-to-all-start.1 = ((bf16[16,128,128]{2,1,0:T(8,128)(2,1)}), bf16[16,128,128]{2,1,0:T(8,128)(2,1)S(1)}, u32[]{:S(2)}, u32[]{:S(2)}) async-start(bf16[16,128,128]{2,1,0:T(8,128)(2,1)} %bitcast.143), calls=%async_computation.1 | async-start | bytes 1048576 | tf_op jit(solution)/shard_map/all_to_all | solution.py:111
  310.3 73.2 %all-reduce.11.cloned.1.call-start = ((), (), s32[]{:S(2)}) async-start(), calls=%async_computation.4 | async-start | bytes 1179648 | tf_op jit(solution)/shard_map/psum | solution.py:123
  319.8 1.2 copy-start.3
  319.8 63.7 %copy-start.2 = (bf16[16,128,128]{2,1,0:T(8,128)(2,1)S(1)}, bf16[16,128,128]{2,1,0:T(8,128)(2,1)}, u32[]{:S(2)}) copy-start(bf16[16,128,128]{2,1,0:T(8,128)(2,1)} %get-tuple-element.229) | copy-start | bytes 1572868
  323.5 208.1 %all-reduce.9.cloned.1.call-start = ((), (), s32[]{:S(2)}) async-start(), calls=%async_computation.3 | async-start | bytes 1179648 | tf_op jit(solution)/shard_map/psum | solution.py:122
Sparse Core Ops, SparseCore 0:
  10.6 143.9 all-gather.1
  323.6 59.7 all-reduce.10
  387.1 144.4 all-reduce.8
